TPU v7x, 32 devices: a whole 2x2x4 slice. The times are simulated.
32 devices in a mesh: dp: 8 (over z, x), mix: 4 (over y, core).
Axes of the slice: x: 2, y: 2, z: 4, core: 2. Of those that a mesh axis runs over, the one named last changes fastest.
Arguments:
- inputs: bfloat16 [40, 1280, 768], P('dp', 'mix'), may hold values from -6 to 6
- pass_count: int32 [40], P('dp'), may hold values from 2 to 5
- pass_embed: bfloat16 [5, 768], replicated, may hold values from -3 to 3
- ln1_gain: bfloat16 [768], replicated, may hold values from 0.5 to 1.5
- ln1_bias: bfloat16 [768], replicated, may hold values from -0.59765625 to 0.59765625
- w_qkv: bfloat16 [768, 2304], replicated, may hold values from -0.21875 to 0.21875
- bias_q: bfloat16 [768], replicated, may hold values from -0.59765625 to 0.59765625
- bias_v: bfloat16 [768], replicated, may hold values from -0.29882812 to 0.29882812
- w_out: bfloat16 [768, 768], replicated, may hold values from -3.5 to 3.5
- bias_out: bfloat16 [768], replicated, may hold values from -0.59765625 to 0.59765625
- ln2_gain: bfloat16 [768], replicated, may hold values from 0.5 to 1.5
- ln2_bias: bfloat16 [768], replicated, may hold values from -0.59765625 to 0.59765625
- w_up: bfloat16 [768, 3072], replicated, may hold values from -0.21875 to 0.21875
- bias_up: bfloat16 [3072], replicated, may hold values from -0.59765625 to 0.59765625
- w_down: bfloat16 [3072, 768], replicated, may hold values from -0.21875 to 0.21875
- bias_down: bfloat16 [768], replicated, may hold values from -0.59765625 to 0.59765625
- cotangent: bfloat16 [40, 1280, 768], P('dp', 'mix'), may hold values from -6 to 6
Outputs:
- out: float32 [40, 1280, 768], P('dp', 'mix')
- grad_x: float32 [40, 1280, 768], P('dp', 'mix')
- grad_pass_embed: float32 [5, 768], replicated
- grad_ln1_gain: float32 [768], replicated
- grad_ln1_bias: float32 [768], replicated
- grad_w_qkv: float32 [768, 2304], P('dp', 'mix')
- grad_bias_q: float32 [768], replicated
- grad_bias_v: float32 [768], replicated
- grad_w_out: float32 [768, 768], P('dp', 'mix')
- grad_bias_out: float32 [768], replicated
- grad_ln2_gain: float32 [768], replicated
- grad_ln2_bias: float32 [768], replicated
- grad_w_up: float32 [768, 3072], P('dp', 'mix')
- grad_bias_up: float32 [3072], replicated
- grad_w_down: float32 [3072, 768], P('dp', 'mix')
- grad_bias_down: float32 [768], replicated
Inputs may be any that keep to these rules, and one draw needn't show every extreme that they name: Item i uses passes 0 to pass_count[i] - 1 of each token; the other slots are masked.
All inputs are finite; a program needn't handle non-finite values.
Results may differ from a plain program's by a relative error of at most 0.0095.
Values may be sent and summed in bfloat16 or wider, within the bound.
No kernel may reach another device: no remote copies, remote signals or barrier semaphores. Data moves between devices by JAX's collectives and lax.ppermute only.
A program may use at most 256 MiB of HBM per device.

v0:
```python
from functools import partial
import math
import jax
import jax.numpy as jnp
from jax import lax
from jax.sharding import PartitionSpec as P

HEAD = 64
PASSES = 5
epsilon = 1e-05
highest = lax.Precision.HIGHEST


def norm_forward(values, gain_vec, shift_vec):
    center = values - jnp.mean(values, axis=-1, keepdims=True)
    inverse = lax.rsqrt(jnp.mean(center * center, axis=-1, keepdims=True) + epsilon)
    normed = center * inverse
    return (normed * gain_vec + shift_vec, normed, inverse)


def norm_backward(upstream, normed, inverse, gain_vec):
    scaled = upstream * gain_vec
    inner_term = scaled - jnp.mean(scaled, axis=-1, keepdims=True)
    inner_term = inner_term - normed * jnp.mean(scaled * normed, axis=-1, keepdims=True)
    return (inverse * inner_term, jnp.sum(upstream * normed, axis=0), jnp.sum(upstream, axis=0))


def split_parts(stacked):
    slot_total = stacked.shape[0]
    heads_dev = stacked.shape[-1] // HEAD
    queries = stacked[:, 0].reshape(slot_total, heads_dev, HEAD)
    key_rows = stacked[:, 1].reshape(slot_total, heads_dev, HEAD)
    value_rows = stacked[:, 2].reshape(slot_total, heads_dev, HEAD)
    return (queries, key_rows, value_rows)


def score_table(queries, key_rows, passes_item):
    slot_total = key_rows.shape[0]
    raw_scores = jnp.einsum("qhd,khd->hqk", queries, key_rows, preferred_element_type=jnp.float32)
    raw_scores = raw_scores * (1.0 / math.sqrt(HEAD))
    slot_ids = lax.iota(jnp.int32, slot_total)
    allowed = (slot_ids[None, :] <= slot_ids[:, None]) & (slot_ids[None, :] % PASSES < passes_item)
    return jnp.where(allowed[None], raw_scores, -1e30)


def attend_item(pieces):
    stacked, passes_item = pieces
    queries, key_rows, value_rows = split_parts(stacked)
    scores = score_table(queries, key_rows, passes_item)
    row_max = jnp.max(scores, axis=-1, keepdims=True)
    log_total = row_max + jnp.log(jnp.sum(jnp.exp(scores - row_max), axis=-1, keepdims=True))
    weights_low = jnp.exp(scores - log_total).astype(jnp.bfloat16)
    attended = jnp.einsum(
        "hqk,khd->qhd", weights_low, value_rows, preferred_element_type=jnp.float32
    )
    return (attended.reshape(stacked.shape[0], -1).astype(jnp.bfloat16), log_total)


def attend_back(pieces):
    stacked, grad_heads, log_total, passes_item = pieces
    queries, key_rows, value_rows = split_parts(stacked)
    slot_total = stacked.shape[0]
    scores = score_table(queries, key_rows, passes_item)
    probs = jnp.exp(scores - log_total)
    grad_part = grad_heads.reshape(slot_total, -1, HEAD)
    grad_probs = jnp.einsum(
        "qhd,khd->hqk", grad_part, value_rows, preferred_element_type=jnp.float32
    )
    row_inner = jnp.sum(probs * grad_probs, axis=-1, keepdims=True)
    grad_scores = (probs * (grad_probs - row_inner)).astype(jnp.bfloat16)
    score_scale = 1.0 / math.sqrt(HEAD)
    grad_query = (
        jnp.einsum("hqk,khd->qhd", grad_scores, key_rows, preferred_element_type=jnp.float32)
        * score_scale
    )
    grad_key = (
        jnp.einsum("hqk,qhd->khd", grad_scores, queries, preferred_element_type=jnp.float32)
        * score_scale
    )
    grad_value = jnp.einsum(
        "hqk,qhd->khd", probs.astype(jnp.bfloat16), grad_part, preferred_element_type=jnp.float32
    )
    joined = jnp.stack([grad_query, grad_key, grad_value], axis=1).astype(jnp.bfloat16)
    return joined.reshape(slot_total, 3, -1)


def per_device(
    inputs,
    pass_count,
    pass_embed,
    ln1_gain,
    ln1_bias,
    w_qkv,
    bias_q,
    bias_v,
    w_out,
    bias_out,
    ln2_gain,
    ln2_bias,
    w_up,
    bias_up,
    w_down,
    bias_down,
    cotangent,
):
    item_dev, slot_dev, model_width = inputs.shape
    row_total = item_dev * slot_dev
    slot_ids = lax.axis_index("mix") * slot_dev + lax.iota(jnp.int32, slot_dev)
    pass_ids = slot_ids % PASSES
    onehot = (pass_ids[:, None] == lax.iota(jnp.int32, PASSES)[None, :]).astype(jnp.float32)
    keep_mask = (pass_ids[None, :] < pass_count[:, None]).astype(jnp.float32).reshape(row_total, 1)
    pass_rows = jnp.dot(onehot, pass_embed.astype(jnp.float32), precision=highest)
    hidden = (inputs.astype(jnp.float32) + pass_rows[None]).reshape(row_total, model_width)
    gain_one = ln1_gain.astype(jnp.float32)
    gain_two = ln2_gain.astype(jnp.float32)
    first, normed_one, inverse_one = norm_forward(hidden, gain_one, ln1_bias.astype(jnp.float32))
    first_low = first.astype(jnp.bfloat16)
    joined_bias = jnp.concatenate(
        [
            bias_q.astype(jnp.float32),
            jnp.zeros((model_width,), jnp.float32),
            bias_v.astype(jnp.float32),
        ]
    )
    joined = jnp.dot(first_low, w_qkv, preferred_element_type=jnp.float32) + joined_bias
    head_block = lax.all_to_all(
        joined.astype(jnp.bfloat16).reshape(item_dev, slot_dev, 3, model_width),
        "mix",
        split_axis=3,
        concat_axis=1,
        tiled=True,
    )
    attended_heads, log_totals = lax.map(attend_item, (head_block, pass_count))
    attended = lax.all_to_all(
        attended_heads, "mix", split_axis=1, concat_axis=2, tiled=True
    ).reshape(row_total, model_width)
    attn_out = jnp.dot(attended, w_out, preferred_element_type=jnp.float32) + bias_out.astype(
        jnp.float32
    )
    mixed_rows = hidden + keep_mask * attn_out
    second, normed_two, inverse_two = norm_forward(
        mixed_rows, gain_two, ln2_bias.astype(jnp.float32)
    )
    second_low = second.astype(jnp.bfloat16)
    pre_act = jnp.dot(second_low, w_up, preferred_element_type=jnp.float32) + bias_up.astype(
        jnp.float32
    )
    act_low = jax.nn.gelu(pre_act, approximate=True).astype(jnp.bfloat16)
    result = mixed_rows + keep_mask * (
        jnp.dot(act_low, w_down, preferred_element_type=jnp.float32) + bias_down.astype(jnp.float32)
    )
    grad_top = cotangent.astype(jnp.float32).reshape(row_total, model_width)
    grad_mlp = (keep_mask * grad_top).astype(jnp.bfloat16)
    grad_wdown = jnp.dot(act_low.T, grad_mlp, preferred_element_type=jnp.float32)
    grad_bdown = jnp.sum(grad_mlp, axis=0, dtype=jnp.float32)
    unused_out, gelu_back = jax.vjp(partial(jax.nn.gelu, approximate=True), pre_act)
    grad_pre = gelu_back(jnp.dot(grad_mlp, w_down.T, preferred_element_type=jnp.float32))[0].astype(
        jnp.bfloat16
    )
    grad_wup = jnp.dot(second_low.T, grad_pre, preferred_element_type=jnp.float32)
    grad_bup = jnp.sum(grad_pre, axis=0, dtype=jnp.float32)
    grad_norm_two, grad_gain_two, grad_shift_two = norm_backward(
        jnp.dot(grad_pre, w_up.T, preferred_element_type=jnp.float32),
        normed_two,
        inverse_two,
        gain_two,
    )
    grad_mixed = grad_top + grad_norm_two
    grad_attn = (keep_mask * grad_mixed).astype(jnp.bfloat16)
    grad_wout = jnp.dot(attended.T, grad_attn, preferred_element_type=jnp.float32)
    grad_bout = jnp.sum(grad_attn, axis=0, dtype=jnp.float32)
    grad_attended = jnp.dot(grad_attn, w_out.T, preferred_element_type=jnp.float32).astype(
        jnp.bfloat16
    )
    grad_attended = grad_attended.reshape(item_dev, slot_dev, model_width)
    grad_heads = lax.all_to_all(grad_attended, "mix", split_axis=2, concat_axis=1, tiled=True)
    grad_stacked = lax.map(attend_back, (head_block, grad_heads, log_totals, pass_count))
    grad_joined = lax.all_to_all(
        grad_stacked, "mix", split_axis=1, concat_axis=3, tiled=True
    ).reshape(row_total, 3 * model_width)
    grad_wqkv = jnp.dot(first_low.T, grad_joined, preferred_element_type=jnp.float32)
    grad_bq = jnp.sum(grad_joined[:, :model_width], axis=0, dtype=jnp.float32)
    grad_bv = jnp.sum(grad_joined[:, 2 * model_width :], axis=0, dtype=jnp.float32)
    grad_norm_one, grad_gain_one, grad_shift_one = norm_backward(
        jnp.dot(grad_joined, w_qkv.T, preferred_element_type=jnp.float32),
        normed_one,
        inverse_one,
        gain_one,
    )
    grad_hidden = grad_mixed + grad_norm_one
    grad_embed = jnp.dot(
        onehot.T,
        jnp.sum(grad_hidden.reshape(item_dev, slot_dev, model_width), axis=0),
        precision=highest,
    )
    partial_sums = (
        lax.psum_scatter(grad_wqkv, "dp", scatter_dimension=0, tiled=True),
        lax.psum_scatter(grad_wout, "dp", scatter_dimension=0, tiled=True),
        lax.psum_scatter(grad_wup, "dp", scatter_dimension=0, tiled=True),
        lax.psum_scatter(grad_wdown, "dp", scatter_dimension=0, tiled=True),
    )
    reduced = (
        lax.psum_scatter(partial_sums[0], "mix", scatter_dimension=1, tiled=True),
        lax.psum_scatter(partial_sums[1], "mix", scatter_dimension=1, tiled=True),
        lax.psum_scatter(partial_sums[2], "mix", scatter_dimension=1, tiled=True),
        lax.psum_scatter(partial_sums[3], "mix", scatter_dimension=1, tiled=True),
    )
    smalls = lax.psum(
        (
            grad_embed,
            grad_gain_one,
            grad_shift_one,
            grad_bq,
            grad_bv,
            grad_bout,
            grad_gain_two,
            grad_shift_two,
            grad_bup,
            grad_bdown,
        ),
        ("dp", "mix"),
    )
    return (
        result.reshape(item_dev, slot_dev, model_width),
        grad_hidden.reshape(item_dev, slot_dev, model_width),
        smalls[0],
        smalls[1],
        smalls[2],
        reduced[0],
        smalls[3],
        smalls[4],
        reduced[1],
        smalls[5],
        smalls[6],
        smalls[7],
        reduced[2],
        smalls[8],
        reduced[3],
        smalls[9],
    )


def solution(mesh):
    return jax.shard_map(
        per_device,
        mesh=mesh,
        in_specs=(
            P("dp", "mix", None),
            P("dp"),
            P(),
            P(),
            P(),
            P(),
            P(),
            P(),
            P(),
            P(),
            P(),
            P(),
            P(),
            P(),
            P(),
            P(),
            P("dp", "mix", None),
        ),
        out_specs=(
            P("dp", "mix", None),
            P("dp", "mix", None),
            P(),
            P(),
            P(),
            P("dp", "mix"),
            P(),
            P(),
            P("dp", "mix"),
            P(),
            P(),
            P(),
            P("dp", "mix"),
            P(),
            P("dp", "mix"),
            P(),
        ),
        check_vma=False,
    )
```

profile of v0, /device:TPU:0, one launch (start us, length us, event | category | flops | bytes accessed | tf_op | source)
XLA Modules:
  0.0 1744.5 jit_solution(5274464120580839720)
XLA Ops:
  39.8 16.9 reshape.398
  56.7 23.4 %copy.79 = bf16[5,320,3,768]{1,2,0,3:T(4,128)(2,1)} copy(bf16[5,320,3,768]{3,2,1,0:T(4,128)(2,1)} %reshape.398) | data formatting | bytes 14745600 | tf_op jit(solution)/shard_map/reshape | solution.py:127
  86.3 130.4 %all-to-all-done = bf16[5,320,3,768]{1,2,0,3:T(4,128)(2,1)} async-done(((bf16[5,320,3,768]{1,2,0,3:T(4,128)(2,1)}), bf16[5,320,3,768]{1,2,0,3:T(4,128)(2,1)}, u32[]{:S(2)}, u32[]{:S(2)}) %all-to-all-start) | async-done | bytes 7372832 | tf_op jit(solution)/shard_map/all_to_all | solution.py:126
  226.0 14.7 copy.81
  240.7 14.7 all_to_all.51
  255.4 182.3 %while.26 = (s32[]{:T(128)}, bf16[5,1280,192]{1,2,0:T(8,128)(2,1)}, f32[5,3,1280,1]{2,1,3,0:T(4,128)}, bf16[5,1280,3,192]{1,3,2,0:T(8,128)(2,1)}, s32[5]{0:T(128)S(1)}, /*index=5*/s32[]{:T(128)}) while((s32[]{:T(128)}, bf16[5,1280,192]{1,2,0:T(8,128)(2,1)}, f32[5,3,1280,1]{2,1,3,0:T(4,128)}, bf16[5,1280,3,192]{1,3,2,0:T(8,128)(2,1)}, ...), condition=%wide.region_5.6_spmd, body=%wide.region_2.5_spmd.sunk | while | flops 1296225280 | bytes 71247464 | solution.py:133
  270.2 9.8 exponential_reduce_fusion.2
  281.4 9.9 fusion.116
  317.8 9.9 fusion.116
  343.1 9.8 exponential_reduce_fusion.2
  354.2 9.9 fusion.116
  390.6 9.9 fusion.116
  427.0 9.9 fusion.116
  465.4 21.5 %all-to-all-done.1 = bf16[4,2,153600]{2,1,0:T(2,128)(2,1)} async-done(((bf16[4,2,153600]{2,1,0:T(2,128)(2,1)}), bf16[4,2,153600]{2,1,0:T(2,128)(2,1)}, u32[]{:S(2)}, u32[]{:S(2)}) %all-to-all-start.1) | async-done | bytes 2457632 | tf_op jit(solution)/shard_map/all_to_all | solution.py:134
  514.5 19.6 %multiply_convert_fusion.1 = (bf16[1600,3072]{1,0:T(8,128)(2,1)}, f32[1600,3072]{1,0:T(8,128)}) fusion(f32[3072]{0:T(1024)S(1)} %copy-done.29, bf16[768,3072]{1,0:T(8,128)(2,1)} %param.33, f32[1600,768]{1,0:T(8,128)S(1)} %get-tuple-element.304, f32[768]{0:T(1024)S(1)} %copy-done.30, f32[768]{0:T(1024)S(1)} %copy-done.28, f32[1600]{0:T(1024)S(1)} %add_rsqrt_fusion.1, ...), kind=kOutput, calls=%fused_computation.53 | convolution fusion | flops 7605043200 | bytes 39156224 | tf_op jit(solution)/shard_map/dot_general | solution.py:145
  534.0 24.4 %convert_reduce_fusion = (f32[3072]{0:T(1024)}, bf16[1600,3072]{1,0:T(8,128)(2,1)}) fusion(f32[1600,3072]{1,0:T(8,128)} %get-tuple-element.306, f32[3072]{0:T(1024)S(1)} %copy-done.29, bf16[1600,768]{1,0:T(8,128)(2,1)S(1)} %copy-done.7, bf16[3072,768]{1,0:T(8,128)(2,1)} %param.35), kind=kOutput, calls=%fused_computation.52 | convolution fusion | flops 7662793728 | bytes 36691968 | tf_op jit(solution)/shard_map/dot_general | solution.py:157
  558.5 15.0 multiply_reduce_fusion.1
  593.9 53.8 %all-to-all-done.2 = bf16[5,320,768]{1,0,2:T(8,128)(2,1)} async-done(((bf16[5,320,768]{1,0,2:T(8,128)(2,1)}), bf16[5,320,768]{1,0,2:T(8,128)(2,1)}, u32[]{:S(2)}, u32[]{:S(2)}) %all-to-all-start.2) | async-done | bytes 2457632 | tf_op jit(solution)/shard_map/all_to_all | solution.py:176
  660.1 286.4 %while.27 = (s32[]{:T(128)}, bf16[5,1280,3,192]{1,3,2,0:T(8,128)(2,1)}, bf16[5,1280,3,192]{1,3,2,0:T(8,128)(2,1)}, s32[5]{0:T(128)S(1)}, f32[5,3,1280,1]{2,1,3,0...) while((s32[]{:T(128)}, bf16[5,1280,3,192]{1,3,2,0:T(8,128)(2,1)}, ...), condition=%wide.region_12.13_spmd, body=%wide.region_10.12_spmd.sunk | while | flops 3198899200 | bytes 167523984 | solution.py:177
  675.1 10.5 fusion.130
  685.6 12.3 multiply_reduce_fusion.10
  698.0 13.2 multiply_convert_fusion.5
  732.4 10.5 fusion.130
  742.9 12.3 multiply_reduce_fusion.10
  755.2 13.2 multiply_convert_fusion.5
  789.7 10.5 fusion.130
  800.2 12.3 multiply_reduce_fusion.10
  812.5 13.2 multiply_convert_fusion.5
  846.9 10.5 fusion.130
  857.4 12.3 multiply_reduce_fusion.10
  869.8 13.2 multiply_convert_fusion.5
  904.2 10.5 fusion.130
  914.7 12.3 multiply_reduce_fusion.10
  927.0 13.2 multiply_convert_fusion.5
  946.5 19.2 %copy.87 = bf16[5,1280,3,192]{3,2,0,1:T(4,128)(2,1)} copy(bf16[5,1280,3,192]{1,3,2,0:T(8,128)(2,1)} %get-tuple-element.163) | data formatting | bytes 14745600 | tf_op jit(solution)/shard_map/while | solution.py:177
  978.6 137.2 %all-to-all-done.3 = bf16[5,1280,3,192]{3,2,0,1:T(4,128)(2,1)} async-done(((bf16[5,1280,3,192]{3,2,0,1:T(4,128)(2,1)}), bf16[5,1280,3,192]{3,2,0,1:T(4,128)(2,1)}, u32[]{:S(2)}, u32[]{:S(2)}) %all-to-all-start.3) | async-done | bytes 7372832 | tf_op jit(solution)/shard_map/all_to_all | solution.py:178
  1115.8 24.6 %copy.103 = bf16[5,4,320,3,192]{4,1,3,2,0:T(4,128)(2,1)} copy(bf16[5,4,320,3,192]{4,3,0,2,1:T(4,128)(2,1)} %bitcast.32) | data formatting | bytes 14745600 | tf_op jit(solution)/shard_map/all_to_all | solution.py:178
  1140.4 16.9 reshape.403
  1157.3 12.1 fusion.47
  1169.7 14.4 fusion.49
  1186.2 16.1 fusion.41
  1202.4 97.4 %reduce-scatter.15.cloned.1.call-done = f32[96,2304]{1,0:T(8,128)} async-done(((f32[768,2304]{1,0:T(8,128)}), f32[96,2304]{1,0:T(8,128)}) %reduce-scatter.15.cloned.1.call-update) | async-done | bytes 884752 | tf_op jit(solution)/shard_map/reduce_scatter | solution.py:197
  1302.5 162.2 %reduce-scatter.23.cloned.1.call-done = f32[384,768]{1,0:T(8,128)} async-done(((f32[3072,768]{1,0:T(8,128)}), f32[384,768]{1,0:T(8,128)}) %reduce-scatter.23.cloned.1.call-update) | async-done | bytes 1179664 | tf_op jit(solution)/shard_map/reduce_scatter | solution.py:200
  1470.4 14.4 multiply_add_fusion.1
  1488.6 164.0 %reduce-scatter.19.cloned.1.call-done = f32[96,3072]{1,0:T(8,128)} async-done(((f32[768,3072]{1,0:T(8,128)}), f32[96,3072]{1,0:T(8,128)}) %reduce-scatter.19.cloned.1.call-update) | async-done | bytes 1179664 | tf_op jit(solution)/shard_map/reduce_scatter | solution.py:199
  1652.6 14.2 multiply_reduce_fusion.2
  1682.4 41.3 %all-reduce = (f32[5,768]{1,0:T(8,128)}, f32[768]{0:T(1024)}, f32[768]{0:T(1024)}, f32[768]{0:T(1024)}, f32[768]{0:T(1024)}, /*index=5*/f32[768]{0:T(1024)}, f32...) all-reduce(f32[5,768]{1,0:T(8,128)} %fusion.34, ...), channel_id=1, replica_groups=mesh['dp'=8,'mix'=4] {'dp','mix'}, use_global_device_ids=true, to_apply=%region_16.17 | all-reduce | flops 13056 | bytes 104448 | tf_op jit(solution)/shard_map/psum | solution.py:208
  1725.6 11.7 reduce-scatter.21.cloned.1.call-done
  (262 shorter events, 399.5 us)
Async XLA Ops:
  7.2 24.1 %copy-start = (bf16[768,2304]{1,0:T(8,128)(2,1)S(1)}, bf16[768,2304]{1,0:T(8,128)(2,1)}, u32[]{:S(2)}) copy-start(bf16[768,2304]{1,0:T(8,128)(2,1)} %param.26) | copy-start | bytes 10616836
  16.8 12.4 copy-start.13
  22.6 6.5 copy-start.25
  22.6 6.5 copy-start.26
  22.6 8.7 copy-start.15
  22.6 8.7 copy-start.17
  22.6 8.7 copy-start.24
  29.1 2.2 copy-start.3
  80.1 136.6 %all-to-all-start = ((bf16[5,320,3,768]{1,2,0,3:T(4,128)(2,1)}), bf16[5,320,3,768]{1,2,0,3:T(4,128)(2,1)}, u32[]{:S(2)}, u32[]{:S(2)}) async-start(bf16[5,320,3,768]{1,2,0,3:T(4,128)(2,1)} %copy.79), calls=%async_computation | async-start | bytes 23592960 | tf_op jit(solution)/shard_map/all_to_all | solution.py:126
  240.7 14.8 copy-start.35
  445.1 12.1 copy-start.32
  445.1 12.7 copy-start.33
  445.1 13.3 copy-start.34
  445.1 13.9 copy-start.22
  452.3 34.5 %all-to-all-start.1 = ((bf16[4,2,153600]{2,1,0:T(2,128)(2,1)}), bf16[4,2,153600]{2,1,0:T(2,128)(2,1)}, u32[]{:S(2)}, u32[]{:S(2)}) async-start(bf16[4,2,153600]{2,1,0:T(2,128)(2,1)} %reshape.412), calls=%async_computation.1 | async-start | bytes 4915200 | tf_op jit(solution)/shard_map/all_to_all | solution.py:134
  459.8 34.3 %copy-start.8 = (f32[5,320]{1,0:T(8,128)}, f32[5,320]{1,0:T(8,128)S(1)}, u32[]{:S(2)}) copy-start(f32[5,320]{1,0:T(8,128)S(1)} %compare_convert_fusion) | copy-start | bytes 19204
  501.1 6.6 copy-start.10
  501.1 6.6 copy-start.31
  513.7 59.8 %copy-start.4 = (f32[1600,768]{1,0:T(8,128)}, f32[1600,768]{1,0:T(8,128)S(1)}, u32[]{:S(2)}) copy-start(f32[1600,768]{1,0:T(8,128)S(1)} %get-tuple-element.304) | copy-start | bytes 14745604
  513.7 59.8 %copy-start.11 = (f32[1600]{0:T(1024)}, f32[1600]{0:T(1024)S(1)}, u32[]{:S(2)}) copy-start(f32[1600]{0:T(1024)S(1)} %broadcast_multiply_fusion.5) | copy-start | bytes 19204
  514.5 59.0 %copy-start.19 = (f32[1600]{0:T(1024)}, f32[1600]{0:T(1024)S(1)}, u32[]{:S(2)}) copy-start(f32[1600]{0:T(1024)S(1)} %add_rsqrt_fusion.1) | copy-start | bytes 19204
  514.5 19.6 %copy-start.7 = (bf16[1600,768]{1,0:T(8,128)(2,1)S(1)}, bf16[1600,768]{1,0:T(8,128)(2,1)}, u32[]{:S(2)}) copy-start(bf16[1600,768]{1,0:T(8,128)(2,1)} %fusion.28) | copy-start | bytes 7372804
  558.5 15.0 copy-start.2
  573.5 5.4 copy-start.37
  578.9 3.6 copy-start.6
  588.9 58.8 %all-to-all-start.2 = ((bf16[5,320,768]{1,0,2:T(8,128)(2,1)}), bf16[5,320,768]{1,0,2:T(8,128)(2,1)}, u32[]{:S(2)}, u32[]{:S(2)}) async-start(bf16[5,320,768]{1,0,2:T(8,128)(2,1)} %copy.84), calls=%async_computation.2 | async-start | bytes 9437184 | tf_op jit(solution)/shard_map/all_to_all | solution.py:176
  647.7 12.4 copy-start.36
  713.0 3.1 copy-start.1
  770.3 3.1 copy-start.1
  827.6 3.1 copy-start.1
  884.8 3.1 copy-start.1
  942.1 3.1 copy-start.1
  965.7 150.1 %all-to-all-start.3 = ((bf16[5,1280,3,192]{3,2,0,1:T(4,128)(2,1)}), bf16[5,1280,3,192]{3,2,0,1:T(4,128)(2,1)}, u32[]{:S(2)}, u32[]{:S(2)}) async-start(bf16[5,1280,3,192]{3,2,0,1:T(4,128)(2,1)} %copy.87), calls=%async_computation.3 | async-start | bytes 26214400 | tf_op jit(solution)/shard_map/all_to_all | solution.py:178
  972.1 212.1 %reduce-scatter.17.cloned.1.call-start = ((), (), s32[]{:S(2)}) async-start(), calls=%async_computation.13 | async-start | bytes 2654208 | tf_op jit(solution)/shard_map/reduce_scatter | solution.py:198
  978.5 321.3 %reduce-scatter.15.cloned.1.call-start = ((), (), s32[]{:S(2)}) async-start(), calls=%async_computation.12 | async-start | bytes 7962624 | tf_op jit(solution)/shard_map/reduce_scatter | solution.py:197
  1169.5 295.2 %reduce-scatter.23.cloned.1.call-start = ((), (), s32[]{:S(2)}) async-start(), calls=%async_computation.16 | async-start | bytes 10616832 | tf_op jit(solution)/shard_map/reduce_scatter | solution.py:200
  1184.1 2.1 copy-start.20
  1184.2 302.8 %reduce-scatter.27.cloned.1.call-start = ((), (), s32[]{:S(2)}) async-start(), calls=%async_computation.18 | async-start | bytes 491520
  1186.1 466.4 %reduce-scatter.19.cloned.1.call-start = ((), (), s32[]{:S(2)}) async-start(), calls=%async_computation.14 | async-start | bytes 10616832 | tf_op jit(solution)/shard_map/reduce_scatter | solution.py:199
  1202.3 265.1 %copy-start.9 = (f32[5,320]{1,0:T(8,128)S(1)}, f32[5,320]{1,0:T(8,128)}, u32[]{:S(2)}) copy-start(f32[5,320]{1,0:T(8,128)} %copy-done.8) | copy-start | bytes 19204
  1202.4 521.4 %reduce-scatter.25.cloned.1.call-start = ((), (), s32[]{:S(2)}) async-start(), calls=%async_computation.17 | async-start | bytes 1474560
  1302.4 423.1 %reduce-scatter.29.cloned.1.call-start = ((), (), s32[]{:S(2)}) async-start(), calls=%async_computation.19 | async-start | bytes 1474560
  1467.4 269.9 %reduce-scatter.21.cloned.1.call-start = ((), (), s32[]{:S(2)}) async-start(), calls=%async_computation.15 | async-start | bytes 1474560 | tf_op jit(solution)/shard_map/reduce_scatter | solution.py:205
  1470.4 182.2 %copy-start.14 = (f32[768]{0:T(1024)S(1)}, f32[768]{0:T(1024)}, u32[]{:S(2)}) copy-start(f32[768]{0:T(1024)} %copy-done.13) | copy-start | bytes 9220
  1470.4 182.2 %copy-start.16 = (f32[1600]{0:T(1024)S(1)}, f32[1600]{0:T(1024)}, u32[]{:S(2)}) copy-start(f32[1600]{0:T(1024)} %div.27) | copy-start | bytes 19204
  1652.6 14.2 copy-start.18
  1673.1 3.8 copy-start.23
  1673.1 9.3 copy-start.27
  (6 other events, 5.9 us)
Sparse Core Ops, SparseCore 0:
  978.7 71.9 reduce-scatter.16
  1169.6 130.1 reduce-scatter.14
  1303.4 161.2 reduce-scatter.22
  1467.0 19.8 reduce-scatter.26
  1490.4 162.0 reduce-scatter.18
  1654.9 24.7 reduce-scatter.24
  1682.8 25.6 reduce-scatter.28
  1711.6 25.5 reduce-scatter.20
where the time goes:
time: 1760 us; the launch traced here: 1740 us
  waiting for transfers between devices  780 us (44%)
  matrix products  436 us (25%)
  local copies, waits for them, and re-layouts  250 us (14%)
  other arithmetic  198 us (11%)
  blocking collectives  41.3 us (2%)
  starting transfers between devices  23.2 us (1%)
    reduce_scatter x1, waiting for transfers between devices, per_device(): lax.psum_scatter(grad_wup, 'dp', scatter_dimension=0, tiled=True)  164 us
    reduce_scatter x1, waiting for transfers between devices, per_device(): lax.psum_scatter(grad_wdown, 'dp', scatter_dimension=0, tiled=True)  162 us
    all_to_all x1, waiting for transfers between devices, per_device(): lax.all_to_all(grad_stacked, 'mix', split_axis=1, concat_axis=3, tiled=True)  137 us
    all_to_all x1, waiting for transfers between devices, per_device(): lax.all_to_all(joined.astype(jnp.bfloat16).reshape(item_dev, slot_dev, 3,...  130 us
    reduce_scatter x1, waiting for transfers between devices, per_device(): lax.psum_scatter(grad_wqkv, 'dp', scatter_dimension=0, tiled=True)  97.4 us
    dot_general x10, matrix products, score_table(): jnp.einsum('qhd,khd->hqk', queries, key_rows, preferred_element_type=jnp....  90 us
    convert_element_type x5, other arithmetic, attend_back(): grad_scores = (probs * (grad_probs - row_inner)).astype(jnp.bfloat16)  66.2 us
    dot_general x5, matrix products, attend_back(): jnp.einsum('qhd,khd->hqk', grad_part, value_rows, preferred_element_type=...  61.7 us
  transfers between devices with their start and end apart: 12, of which 9 were waited for; matrix products, arithmetic and copies ran while one was open for 9% of the time, Pallas kernels for 0%

commit v1 on v0

--- a/solution.py
+++ b/solution.py
@@ -9,6 +9,18 @@
 PASSES = 5
 epsilon = 1e-05
 highest = lax.Precision.HIGHEST
+
+
+def cut_along(x, dim, length):
+    shape = x.shape
+    tiles = x.reshape(*shape[:dim], length, shape[dim] // length, *shape[dim + 1 :])
+    return jnp.moveaxis(tiles, dim, 0)
+
+
+def joined_along(blocks, dim):
+    lengths = list(blocks.shape[1:])
+    lengths[dim] *= blocks.shape[0]
+    return jnp.moveaxis(blocks, 0, dim).reshape(lengths)
 
 
 def norm_forward(values, gain_vec, shift_vec):
@@ -123,13 +135,15 @@
         ]
     )
     joined = jnp.dot(first_low, w_qkv, preferred_element_type=jnp.float32) + joined_bias
-    head_block = lax.all_to_all(
-        joined.astype(jnp.bfloat16).reshape(item_dev, slot_dev, 3, model_width),
-        "mix",
-        split_axis=3,
-        concat_axis=1,
-        tiled=True,
-    )
+    array = joined.astype(jnp.bfloat16).reshape(item_dev, slot_dev, 3, model_width)
+    size, mine = (lax.axis_size("mix"), lax.axis_index("mix"))
+    blocks = cut_along(array, 3, size)
+    finished = [blocks[mine]]
+    for step in range(1, size):
+        sent = blocks[mine ^ step]
+        finished.append(lax.ppermute(sent, "mix", [(i, i ^ step) for i in range(size)]))
+    blocks = jnp.stack(finished)[mine ^ jnp.arange(size)]
+    head_block = joined_along(blocks, 1)
     attended_heads, log_totals = lax.map(attend_item, (head_block, pass_count))
     attended = lax.all_to_all(
         attended_heads, "mix", split_axis=1, concat_axis=2, tiled=True

time: 1760 us -> 1790 us (1.017)
  local copies, waits for them, and re-layouts: 250 us -> 317 us
  waiting for transfers between devices: 780 us -> 725 us
  other arithmetic: 198 us -> 217 us
    all_to_all x1 -> x0, waiting for transfers between devices: 130 us -> none  [per_device(): lax.all_to_all(joined.astype(jnp.bfloat16).reshape(item_dev, slot_dev, 3,...]
    another operation x0 -> x6, local copies, waits for them, and re-layouts: none -> 91.9 us
    ppermute x0 -> x3, waiting for transfers between devices: none -> 75.5 us  [per_device(): lax.ppermute(sent, 'mix', [(i, i ^ step) for i in range(size)])]
    all_to_all x3 -> x0, local copies, waits for them, and re-layouts: 38.8 us -> none  [per_device(): lax.all_to_all(joined.astype(jnp.bfloat16).reshape(item_dev, slot_dev, 3,...]
    reshape x2 -> x1, local copies, waits for them, and re-layouts: 40.3 us -> 14.8 us  [joined_along(): return jnp.moveaxis(blocks, 0, dim).reshape(lengths)]
    gather x0 -> x5, local copies, waits for them, and re-layouts: none -> 24.8 us  [per_device(): blocks = jnp.stack(finished)[mine ^ jnp.arange(size)]]
  transfers between devices with their start and end apart: 12 -> 14, of which waited for: 9 -> 10; matrix products, arithmetic and copies ran while one was open for 9% -> 11% of each run, Pallas kernels for 0% -> 0%
where the time goes in v1:
time: 1790 us; the launch traced here: 1770 us
  waiting for transfers between devices  725 us (41%)
  matrix products  436 us (24%)
  local copies, waits for them, and re-layouts  317 us (18%)
  other arithmetic  217 us (12%)
  blocking collectives  41.3 us (2%)
  starting transfers between devices  19.9 us (1%)
    reduce_scatter x1, waiting for transfers between devices, per_device(): lax.psum_scatter(grad_wup, 'dp', scatter_dimension=0, tiled=True)  164 us
    reduce_scatter x1, waiting for transfers between devices, per_device(): lax.psum_scatter(grad_wdown, 'dp', scatter_dimension=0, tiled=True)  162 us
    all_to_all x1, waiting for transfers between devices, per_device(): lax.all_to_all(grad_stacked, 'mix', split_axis=1, concat_axis=3, tiled=True)  137 us
    reduce_scatter x1, waiting for transfers between devices, per_device(): lax.psum_scatter(grad_wqkv, 'dp', scatter_dimension=0, tiled=True)  96.7 us
    dot_general x10, matrix products, score_table(): jnp.einsum('qhd,khd->hqk', queries, key_rows, preferred_element_type=jnp....  90.2 us
    ppermute x3, waiting for transfers between devices, per_device(): lax.ppermute(sent, 'mix', [(i, i ^ step) for i in range(size)])  75.5 us
    another operation x5, local copies, waits for them, and re-layouts  72.9 us
    convert_element_type x5, other arithmetic, attend_back(): grad_scores = (probs * (grad_probs - row_inner)).astype(jnp.bfloat16)  66.2 us
  transfers between devices with their start and end apart: 14, of which 10 were waited for; matrix products, arithmetic and copies ran while one was open for 11% of the time, Pallas kernels for 0%

profile of v1, /device:TPU:0, one launch (start us, length us, event | category | flops | bytes accessed | tf_op | source)
XLA Modules:
  0.0 1772.1 jit_solution(5453899505522165566)
XLA Ops:
  39.8 19.0 %reshape_reshape.3 = bf16[5,320,3,4,192]{4,3,2,1,0:T(4,128)(2,1)} reshape(bf16[1600,2304]{1,0:T(8,128)(2,1)} %add_convert_fusion) | data formatting | bytes 14745600 | tf_op jit(solution)/shard_map/reshape;reshape | solution.py:16
  58.8 31.7 %constant_dynamic-slice_fusion.4 = (bf16[5,320,3,1,192]{4,3,2,1,0:T(2,128)(2,1)}, bf16[5,320,3,1,192]{4,3,2,1,0:T(2,128)(2,1)}, bf16[5,320,3,1,192]{4,3,2,1,0:T(2,128)(2,1)}, bf16[5,320,3,1,192]{4,3,2,1,0:T(2,128)(2,1)}) fusion(bf16[5,320,3,4,192]{4,3,2,1,0:T(4,128)(2,1)} %reshape_reshape.3, s32[]{:T(128)S(6)} %select_n.81, s32[]{:T(128)S(6)} %select_n.84, ...), kind=kLoop, calls=%fused_computation.120 | loop fusion | bytes 14745616 | tf_op jit(solution)/shard_map/dynamic-slice
  90.5 10.3 copy.74
  101.3 10.3 copy.75
  114.0 10.3 copy.76
  124.5 10.3 copy.73
  134.8 28.5 %collective-permute-done.1 = bf16[5,320,3,192]{1,3,2,0:T(8,128)(2,1)} collective-permute-done((bf16[5,320,3,192]{1,3,2,0:T(8,128)(2,1)}, bf16[5,320,3,192]{1,3,2,0:T(8,128)(2,1)}, u32[]{:S(2)}, u32[]{:S(2)}) %collective-permute-start.1) | collective-permute-done | bytes 1843232 | tf_op jit(solution)/shard_map/ppermute | solution.py:144
  163.3 47.0 %collective-permute-done.2 = bf16[5,320,3,192]{1,3,2,0:T(8,128)(2,1)} collective-permute-done((bf16[5,320,3,192]{1,3,2,0:T(8,128)(2,1)}, bf16[5,320,3,192]{1,3,2,0:T(8,128)(2,1)}, u32[]{:S(2)}, u32[]{:S(2)}) %collective-permute-start.2) | collective-permute-done | bytes 1843232 | tf_op jit(solution)/shard_map/ppermute | solution.py:144
  254.6 14.7 copy.79
  269.3 14.8 reshape.421
  284.0 182.2 %while.26 = (s32[]{:T(128)}, bf16[5,1280,192]{1,2,0:T(8,128)(2,1)}, f32[5,3,1280,1]{2,1,3,0:T(4,128)}, bf16[5,1280,3,192]{1,3,2,0:T(8,128)(2,1)}, s32[5]{0:T(128)S(1)}, /*index=5*/s32[]{:T(128)}) while((s32[]{:T(128)}, bf16[5,1280,192]{1,2,0:T(8,128)(2,1)}, f32[5,3,1280,1]{2,1,3,0:T(4,128)}, bf16[5,1280,3,192]{1,3,2,0:T(8,128)(2,1)}, ...), condition=%wide.region_5.6_spmd, body=%wide.region_2.5_spmd.sunk | while | flops 1296225280 | bytes 71247464 | solution.py:147
  346.2 9.9 fusion.117
  419.1 9.9 fusion.117
  493.6 21.5 %all-to-all-done = bf16[4,2,153600]{2,1,0:T(2,128)(2,1)} async-done(((bf16[4,2,153600]{2,1,0:T(2,128)(2,1)}), bf16[4,2,153600]{2,1,0:T(2,128)(2,1)}, u32[]{:S(2)}, u32[]{:S(2)}) %all-to-all-start) | async-done | bytes 2457632 | tf_op jit(solution)/shard_map/all_to_all | solution.py:148
  542.8 19.6 %multiply_convert_fusion.1 = (bf16[1600,3072]{1,0:T(8,128)(2,1)}, f32[1600,3072]{1,0:T(8,128)}) fusion(f32[3072]{0:T(1024)S(1)} %copy-done.30, bf16[768,3072]{1,0:T(8,128)(2,1)} %param.33, f32[1600,768]{1,0:T(8,128)S(1)} %get-tuple-element.292, f32[768]{0:T(1024)S(1)} %copy-done.31, f32[768]{0:T(1024)S(1)} %copy-done.29, f32[1600]{0:T(1024)S(1)} %add_rsqrt_fusion.1, ...), kind=kOutput, calls=%fused_computation.55 | convolution fusion | flops 7605043200 | bytes 39156224 | tf_op jit(solution)/shard_map/dot_general | solution.py:159
  562.4 24.7 %convert_reduce_fusion = (f32[3072]{0:T(1024)}, bf16[1600,3072]{1,0:T(8,128)(2,1)}) fusion(f32[1600,3072]{1,0:T(8,128)} %get-tuple-element.294, f32[3072]{0:T(1024)S(1)} %copy-done.30, bf16[1600,768]{1,0:T(8,128)(2,1)S(1)} %copy-done.8, bf16[3072,768]{1,0:T(8,128)(2,1)} %param.35), kind=kOutput, calls=%fused_computation.54 | convolution fusion | flops 7662793728 | bytes 36691968 | tf_op jit(solution)/shard_map/dot_general | solution.py:171
  587.0 15.0 multiply_reduce_fusion.1
  622.2 53.8 %all-to-all-done.1 = bf16[5,320,768]{1,0,2:T(8,128)(2,1)} async-done(((bf16[5,320,768]{1,0,2:T(8,128)(2,1)}), bf16[5,320,768]{1,0,2:T(8,128)(2,1)}, u32[]{:S(2)}, u32[]{:S(2)}) %all-to-all-start.1) | async-done | bytes 2457632 | tf_op jit(solution)/shard_map/all_to_all | solution.py:190
  688.4 286.4 %while.27 = (s32[]{:T(128)}, bf16[5,1280,3,192]{1,3,2,0:T(8,128)(2,1)}, bf16[5,1280,3,192]{1,3,2,0:T(8,128)(2,1)}, s32[5]{0:T(128)S(1)}, f32[5,3,1280,1]{2,1,3,0...) while((s32[]{:T(128)}, bf16[5,1280,3,192]{1,3,2,0:T(8,128)(2,1)}, ...), condition=%wide.region_12.13_spmd, body=%wide.region_10.12_spmd.sunk | while | flops 3198899200 | bytes 167523984 | solution.py:191
  703.5 10.5 fusion.131
  714.0 12.3 multiply_reduce_fusion.10
  726.3 13.2 multiply_convert_fusion.5
  760.8 10.5 fusion.131
  771.3 12.3 multiply_reduce_fusion.10
  783.6 13.2 multiply_convert_fusion.5
  818.0 10.5 fusion.131
  828.5 12.3 multiply_reduce_fusion.10
  840.9 13.2 multiply_convert_fusion.5
  875.3 10.5 fusion.131
  885.8 12.3 multiply_reduce_fusion.10
  898.1 13.2 multiply_convert_fusion.5
  932.6 10.5 fusion.131
  943.1 12.3 multiply_reduce_fusion.10
  955.4 13.2 multiply_convert_fusion.5
  974.8 19.3 %copy.85 = bf16[5,1280,3,192]{3,2,0,1:T(4,128)(2,1)} copy(bf16[5,1280,3,192]{1,3,2,0:T(8,128)(2,1)} %get-tuple-element.163) | data formatting | bytes 14745600 | tf_op jit(solution)/shard_map/while | solution.py:191
  1007.2 137.0 %all-to-all-done.2 = bf16[5,1280,3,192]{3,2,0,1:T(4,128)(2,1)} async-done(((bf16[5,1280,3,192]{3,2,0,1:T(4,128)(2,1)}), bf16[5,1280,3,192]{3,2,0,1:T(4,128)(2,1)}, u32[]{:S(2)}, u32[]{:S(2)}) %all-to-all-start.2) | async-done | bytes 7372832 | tf_op jit(solution)/shard_map/all_to_all | solution.py:192
  1144.2 24.6 %copy.101 = bf16[5,4,320,3,192]{4,1,3,2,0:T(4,128)(2,1)} copy(bf16[5,4,320,3,192]{4,3,0,2,1:T(4,128)(2,1)} %bitcast.39) | data formatting | bytes 14745600 | tf_op jit(solution)/shard_map/all_to_all | solution.py:192
  1168.8 16.9 reshape.426
  1185.7 12.2 fusion.48
  1198.1 14.4 fusion.50
  1214.6 16.0 fusion.42
  1230.7 96.7 %reduce-scatter.15.cloned.1.call-done = f32[96,2304]{1,0:T(8,128)} async-done(((f32[768,2304]{1,0:T(8,128)}), f32[96,2304]{1,0:T(8,128)}) %reduce-scatter.15.cloned.1.call-update) | async-done | bytes 884752 | tf_op jit(solution)/shard_map/reduce_scatter | solution.py:211
  1330.1 162.2 %reduce-scatter.23.cloned.1.call-done = f32[384,768]{1,0:T(8,128)} async-done(((f32[3072,768]{1,0:T(8,128)}), f32[384,768]{1,0:T(8,128)}) %reduce-scatter.23.cloned.1.call-update) | async-done | bytes 1179664 | tf_op jit(solution)/shard_map/reduce_scatter | solution.py:214
  1498.0 14.4 multiply_add_fusion.1
  1516.2 163.9 %reduce-scatter.19.cloned.1.call-done = f32[96,3072]{1,0:T(8,128)} async-done(((f32[768,3072]{1,0:T(8,128)}), f32[96,3072]{1,0:T(8,128)}) %reduce-scatter.19.cloned.1.call-update) | async-done | bytes 1179664 | tf_op jit(solution)/shard_map/reduce_scatter | solution.py:213
  1680.2 14.2 multiply_reduce_fusion.2
  1710.0 41.3 %all-reduce = (f32[5,768]{1,0:T(8,128)}, f32[768]{0:T(1024)}, f32[768]{0:T(1024)}, f32[768]{0:T(1024)}, f32[768]{0:T(1024)}, /*index=5*/f32[768]{0:T(1024)}, f32...) all-reduce(f32[5,768]{1,0:T(8,128)} %fusion.34, ...), channel_id=1, replica_groups=mesh['dp'=8,'mix'=4] {'dp','mix'}, use_global_device_ids=true, to_apply=%region_16.17 | all-reduce | flops 13056 | bytes 104448 | tf_op jit(solution)/shard_map/psum | solution.py:222
  1753.2 11.7 reduce-scatter.21.cloned.1.call-done
  (281 shorter events, 480.5 us)
Async XLA Ops:
  7.2 24.1 %copy-start = (bf16[768,2304]{1,0:T(8,128)(2,1)S(1)}, bf16[768,2304]{1,0:T(8,128)(2,1)}, u32[]{:S(2)}) copy-start(bf16[768,2304]{1,0:T(8,128)(2,1)} %param.26) | copy-start | bytes 10616836
  16.8 12.3 copy-start.14
  22.6 6.5 copy-start.26
  22.6 6.5 copy-start.27
  22.6 8.7 copy-start.16
  22.6 8.7 copy-start.18
  22.6 8.7 copy-start.25
  100.8 34.0 %collective-permute-start = (bf16[5,320,3,192]{1,3,2,0:T(8,128)(2,1)}, bf16[5,320,3,192]{1,3,2,0:T(8,128)(2,1)}, u32[]{:S(2)}, u32[]{:S(2)}) collective-permute-start(bf16[5,320,3,192]{1,3,2,0:T(8,128)(2,1)} %bitcast.198), channel_id=1, source_target_pairs={{0,1},{1,0},{2,3},{3,2},{4,5},{5,4},{6,7},{7,6},{8,9},{9,8},{10,11... | collective-permute-start | bytes 5529608 | tf_op jit(solution)/shard_map/ppermute | solution.py:144
  111.5 51.8 %collective-permute-start.1 = (bf16[5,320,3,192]{1,3,2,0:T(8,128)(2,1)}, bf16[5,320,3,192]{1,3,2,0:T(8,128)(2,1)}, u32[]{:S(2)}, u32[]{:S(2)}) collective-permute-start(bf16[5,320,3,192]{1,3,2,0:T(8,128)(2,1)} %bitcast.199), channel_id=1, source_target_pairs={{0,2},{1,3},{2,0},{3,1},{4,6},{5,7},{6,4},{7,5},{8,10},{9,11},{10,... | collective-permute-start | bytes 5529608 | tf_op jit(solution)/shard_map/ppermute | solution.py:144
  124.3 86.0 %collective-permute-start.2 = (bf16[5,320,3,192]{1,3,2,0:T(8,128)(2,1)}, bf16[5,320,3,192]{1,3,2,0:T(8,128)(2,1)}, u32[]{:S(2)}, u32[]{:S(2)}) collective-permute-start(bf16[5,320,3,192]{1,3,2,0:T(8,128)(2,1)} %bitcast.200), channel_id=1, source_target_pairs={{0,3},{1,2},{2,1},{3,0},{4,7},{5,6},{6,5},{7,4},{8,11},{9,10},{10,... | collective-permute-start | bytes 5529608 | tf_op jit(solution)/shard_map/ppermute | solution.py:144
  210.3 3.4 copy-start.3
  269.3 14.8 copy-start.36
  473.8 11.7 copy-start.33
  473.8 12.3 copy-start.34
  473.8 12.9 copy-start.35
  473.8 13.5 copy-start.23
  481.0 34.1 %all-to-all-start = ((bf16[4,2,153600]{2,1,0:T(2,128)(2,1)}), bf16[4,2,153600]{2,1,0:T(2,128)(2,1)}, u32[]{:S(2)}, u32[]{:S(2)}) async-start(bf16[4,2,153600]{2,1,0:T(2,128)(2,1)} %reshape.451), calls=%async_computation | async-start | bytes 4915200 | tf_op jit(solution)/shard_map/all_to_all | solution.py:148
  488.1 34.3 %copy-start.9 = (f32[5,320]{1,0:T(8,128)}, f32[5,320]{1,0:T(8,128)S(1)}, u32[]{:S(2)}) copy-start(f32[5,320]{1,0:T(8,128)S(1)} %compare_convert_fusion) | copy-start | bytes 19204
  529.4 6.6 copy-start.11
  529.4 6.6 copy-start.32
  542.0 60.1 %copy-start.5 = (f32[1600,768]{1,0:T(8,128)}, f32[1600,768]{1,0:T(8,128)S(1)}, u32[]{:S(2)}) copy-start(f32[1600,768]{1,0:T(8,128)S(1)} %get-tuple-element.292) | copy-start | bytes 14745604
  542.0 60.0 %copy-start.12 = (f32[1600]{0:T(1024)}, f32[1600]{0:T(1024)S(1)}, u32[]{:S(2)}) copy-start(f32[1600]{0:T(1024)S(1)} %broadcast_multiply_fusion.5) | copy-start | bytes 19204
  542.8 59.3 %copy-start.20 = (f32[1600]{0:T(1024)}, f32[1600]{0:T(1024)S(1)}, u32[]{:S(2)}) copy-start(f32[1600]{0:T(1024)S(1)} %add_rsqrt_fusion.1) | copy-start | bytes 19204
  542.8 19.6 %copy-start.8 = (bf16[1600,768]{1,0:T(8,128)(2,1)S(1)}, bf16[1600,768]{1,0:T(8,128)(2,1)}, u32[]{:S(2)}) copy-start(bf16[1600,768]{1,0:T(8,128)(2,1)} %fusion.28) | copy-start | bytes 7372804
  587.0 15.0 copy-start.2
  602.1 5.2 copy-start.38
  607.3 3.6 copy-start.7
  617.3 58.8 %all-to-all-start.1 = ((bf16[5,320,768]{1,0,2:T(8,128)(2,1)}), bf16[5,320,768]{1,0,2:T(8,128)(2,1)}, u32[]{:S(2)}, u32[]{:S(2)}) async-start(bf16[5,320,768]{1,0,2:T(8,128)(2,1)} %copy.82), calls=%async_computation.1 | async-start | bytes 9437184 | tf_op jit(solution)/shard_map/all_to_all | solution.py:190
  676.0 12.4 copy-start.37
  741.4 3.1 copy-start.1
  798.7 3.1 copy-start.1
  855.9 3.1 copy-start.1
  913.2 3.1 copy-start.1
  994.1 150.1 %all-to-all-start.2 = ((bf16[5,1280,3,192]{3,2,0,1:T(4,128)(2,1)}), bf16[5,1280,3,192]{3,2,0,1:T(4,128)(2,1)}, u32[]{:S(2)}, u32[]{:S(2)}) async-start(bf16[5,1280,3,192]{3,2,0,1:T(4,128)(2,1)} %copy.85), calls=%async_computation.2 | async-start | bytes 26214400 | tf_op jit(solution)/shard_map/all_to_all | solution.py:192
  1000.5 212.1 %reduce-scatter.17.cloned.1.call-start = ((), (), s32[]{:S(2)}) async-start(), calls=%async_computation.12 | async-start | bytes 2654208 | tf_op jit(solution)/shard_map/reduce_scatter | solution.py:212
  1007.2 320.3 %reduce-scatter.15.cloned.1.call-start = ((), (), s32[]{:S(2)}) async-start(), calls=%async_computation.11 | async-start | bytes 7962624 | tf_op jit(solution)/shard_map/reduce_scatter | solution.py:211
  1197.9 294.4 %reduce-scatter.23.cloned.1.call-start = ((), (), s32[]{:S(2)}) async-start(), calls=%async_computation.15 | async-start | bytes 10616832 | tf_op jit(solution)/shard_map/reduce_scatter | solution.py:214
  1212.5 302.1 %reduce-scatter.27.cloned.1.call-start = ((), (), s32[]{:S(2)}) async-start(), calls=%async_computation.17 | async-start | bytes 491520
  1214.5 465.6 %reduce-scatter.19.cloned.1.call-start = ((), (), s32[]{:S(2)}) async-start(), calls=%async_computation.13 | async-start | bytes 10616832 | tf_op jit(solution)/shard_map/reduce_scatter | solution.py:213
  1230.7 264.4 %copy-start.10 = (f32[5,320]{1,0:T(8,128)S(1)}, f32[5,320]{1,0:T(8,128)}, u32[]{:S(2)}) copy-start(f32[5,320]{1,0:T(8,128)} %copy-done.9) | copy-start | bytes 19204
  1230.7 520.7 %reduce-scatter.25.cloned.1.call-start = ((), (), s32[]{:S(2)}) async-start(), calls=%async_computation.16 | async-start | bytes 1474560
  1330.1 423.1 %reduce-scatter.29.cloned.1.call-start = ((), (), s32[]{:S(2)}) async-start(), calls=%async_computation.18 | async-start | bytes 1474560
  1495.0 269.9 %reduce-scatter.21.cloned.1.call-start = ((), (), s32[]{:S(2)}) async-start(), calls=%async_computation.14 | async-start | bytes 1474560 | tf_op jit(solution)/shard_map/reduce_scatter | solution.py:219
  1498.0 182.2 %copy-start.15 = (f32[768]{0:T(1024)S(1)}, f32[768]{0:T(1024)}, u32[]{:S(2)}) copy-start(f32[768]{0:T(1024)} %copy-done.14) | copy-start | bytes 9220
  1498.0 182.2 %copy-start.17 = (f32[1600]{0:T(1024)S(1)}, f32[1600]{0:T(1024)}, u32[]{:S(2)}) copy-start(f32[1600]{0:T(1024)} %div.27) | copy-start | bytes 19204
  1680.2 14.2 copy-start.19
  1700.8 3.8 copy-start.24
  1700.8 9.2 copy-start.28
  (9 other events, 13.3 us)
Sparse Core Ops, SparseCore 0:
  1007.3 71.1 reduce-scatter.16
  1198.0 129.3 reduce-scatter.14
  1331.1 161.2 reduce-scatter.22
  1494.7 19.9 reduce-scatter.26
  1518.1 162.0 reduce-scatter.18
  1682.6 24.6 reduce-scatter.24
  1710.5 25.6 reduce-scatter.28
  1739.2 25.6 reduce-scatter.20
